TPU v7x, 32 devices: a whole 2x2x4 slice. The times are simulated.
32 devices in a mesh: pb: 2 (over x), ka: 16 (over z, y, core).
Axes of the slice: x: 2, y: 2, z: 4, core: 2. Of those that a mesh axis runs over, the one named last changes fastest.
Arguments:
- coupling: bfloat16 [5120, 2, 2048], P('ka', 'pb'), may hold values from -0.009765625 to 0.009765625
- eigvec: float32 [16, 2048], P('ka'), may hold values from -0.75 to 0.75
- energies: float32 [16, 32], P('ka'), may hold values from -1 to 1
- k_coords: int32 [3, 16], replicated, may hold values from 0 to 63
- r_coords: int32 [3, 5120], P(None, 'ka'), may hold values from -12 to 12
- degeneracy: int32 [5120], P('ka'), may hold values from 1 to 8
- kq_index: int32 [16, 24], P('ka', 'pb'), may hold values from 0 to 15
- omega: float32 [24, 2], P('pb'), may hold values from 0.05 to 0.5
- phonon_modes: float32 [24, 2, 2], P('pb'), may hold values from -4 to 4
Outputs:
- sigma: float32 [16, 32], P('ka', 'pb')
All inputs are finite; a program needn't handle non-finite values.
Results may differ from a plain program's by a relative error of at most 0.0013.
Values may be sent and summed in bfloat16 or wider, within the bound.
No kernel may reach another device: no remote copies, remote signals or barrier semaphores. Data moves between devices by JAX's collectives and lax.ppermute only.
A program may use at most 64 MiB of HBM per device.

v0:
```python
import math
import jax
import jax.numpy as jnp
from jax import lax
from jax.sharding import PartitionSpec as P

KGRID = 64
THERMAL = 0.1
SMEARING = 0.05
HIGHEST = lax.Precision.HIGHEST


def phases(k_coords, r_coords, degeneracy):
    turns = (
        k_coords[0][:, None] * r_coords[0][None, :]
        + k_coords[1][:, None] * r_coords[1][None, :]
        + k_coords[2][:, None] * r_coords[2][None, :]
    ) % KGRID
    angle = turns.astype(jnp.float32) * (2.0 * math.pi / KGRID)
    inverse = 1.0 / degeneracy.astype(jnp.float32)
    cosine = (jnp.cos(angle) * inverse[None, :]).astype(jnp.bfloat16)
    sine = (jnp.sin(angle) * inverse[None, :]).astype(jnp.bfloat16)
    return (cosine, sine)


def combine_parts(cosine_sum, sine_sum, modes, square):
    cosine_rows = cosine_sum.reshape(cosine_sum.shape[0], modes, 2, square)
    sine_rows = sine_sum.reshape(sine_sum.shape[0], modes, 2, square)
    real_part = cosine_rows[:, :, 0] - sine_rows[:, :, 1]
    imag_part = cosine_rows[:, :, 1] + sine_rows[:, :, 0]
    return jnp.stack([real_part, imag_part], axis=2).reshape(
        cosine_sum.shape[0], modes * 2 * square
    )


def lorentz(spacing):
    return SMEARING / (math.pi * (spacing * spacing + SMEARING * SMEARING))


def self_energy(wannier, vector, energy, kq_vectors, kq_energies, omega, phonon):
    bands = energy.shape[0]
    modes = wannier.shape[0]
    matrix = wannier.astype(jnp.float32).reshape(modes, 2, bands, bands)
    rotate = vector.reshape(2, bands, bands)
    fold_real = jnp.einsum("vac,cn->van", matrix[:, 0], rotate[0], precision=HIGHEST) - jnp.einsum(
        "vac,cn->van", matrix[:, 1], rotate[1], precision=HIGHEST
    )
    fold_imag = jnp.einsum("vac,cn->van", matrix[:, 0], rotate[1], precision=HIGHEST) + jnp.einsum(
        "vac,cn->van", matrix[:, 1], rotate[0], precision=HIGHEST
    )
    mixed_real = jnp.einsum("qwv,wan->qvan", phonon, fold_real, precision=HIGHEST)
    mixed_imag = jnp.einsum("qwv,wan->qvan", phonon, fold_imag, precision=HIGHEST)
    target = kq_vectors.reshape(-1, 2, bands, bands)
    final_real = jnp.einsum(
        "qam,qvan->qmvn", target[:, 0], mixed_real, precision=HIGHEST
    ) + jnp.einsum("qam,qvan->qmvn", target[:, 1], mixed_imag, precision=HIGHEST)
    final_imag = jnp.einsum(
        "qam,qvan->qmvn", target[:, 0], mixed_imag, precision=HIGHEST
    ) - jnp.einsum("qam,qvan->qmvn", target[:, 1], mixed_real, precision=HIGHEST)
    strength = final_real * final_real + final_imag * final_imag
    fermi = 1.0 / (1.0 + jnp.exp(kq_energies / THERMAL))
    bose = 1.0 / jnp.expm1(omega / THERMAL)
    spacing = energy[None, None, None, :] - kq_energies[:, :, None, None]
    absorb = lorentz(spacing + omega[:, None, :, None])
    emit = lorentz(spacing - omega[:, None, :, None])
    bose_wide = bose[:, None, :, None]
    fermi_wide = fermi[:, :, None, None]
    occupy = (bose_wide + fermi_wide) * absorb + (bose_wide + 1.0 - fermi_wide) * emit
    return jnp.sum(strength * occupy, axis=(0, 1, 2))


def fourier_terms(k_coords, r_coords, degeneracy, slab, modes, square, count):
    cosine, sine = phases(k_coords, r_coords, degeneracy)
    stacked = jnp.dot(
        jnp.concatenate([cosine, sine], axis=0), slab, preferred_element_type=jnp.float32
    )
    return combine_parts(stacked[:count], stacked[count:], modes, square)


def shards(
    coupling, eigvec, energies, k_coords, r_coords, degeneracy, kq_index, omega, phonon_modes
):
    bands = energies.shape[1]
    points = eigvec.shape[0]
    local_modes = coupling.shape[1]
    slab = coupling.reshape(coupling.shape[0], -1)
    partial_value = lax.psum_scatter(
        fourier_terms(
            k_coords,
            r_coords,
            degeneracy,
            slab,
            local_modes,
            bands * bands,
            points * lax.axis_size("ka"),
        ),
        "ka",
        scatter_dimension=0,
        tiled=True,
    )
    own_wannier = partial_value.astype(jnp.bfloat16).reshape(points, local_modes, 2 * bands * bands)
    wannier = lax.all_gather(own_wannier, "pb", axis=1, tiled=True)
    pairs = kq_index.reshape(-1)
    pieces = (
        lax.all_gather(eigvec, "ka", axis=0, tiled=True),
        lax.all_gather(energies, "ka", axis=0, tiled=True),
    )
    labels = jnp.arange(pieces[0].shape[0], dtype=jnp.int32)
    hits = (pairs[:, None] == labels[None, :]).astype(jnp.float32)
    vectors_sum = jnp.dot(hits, pieces[0], precision=HIGHEST, preferred_element_type=jnp.float32)
    energy_sum = jnp.dot(hits, pieces[1], precision=HIGHEST, preferred_element_type=jnp.float32)
    kq_vectors = vectors_sum
    kq_energies = energy_sum
    queries = kq_index.shape[1]
    kq_vectors = kq_vectors.reshape(points, queries, eigvec.shape[1])
    kq_energies = kq_energies.reshape(points, queries, bands)

    def per_point(items):
        wannier_row, vector, energy, kq_rows, kq_levels = items
        return self_energy(wannier_row, vector, energy, kq_rows, kq_levels, omega, phonon_modes)

    sigma = lax.map(per_point, (wannier, eigvec, energies, kq_vectors, kq_energies))
    sigma = sigma / (queries * lax.axis_size("pb"))
    return lax.psum_scatter(sigma, "pb", scatter_dimension=1, tiled=True)


def solution(mesh):
    in_specs = (
        P("ka", "pb", None),
        P("ka", None),
        P("ka", None),
        P(),
        P(None, "ka"),
        P("ka"),
        P("ka", "pb"),
        P("pb", None),
        P("pb", None, None),
    )
    out_specs = P("ka", "pb")
    return jax.shard_map(shards, mesh=mesh, in_specs=in_specs, out_specs=out_specs, check_vma=False)
```

profile of v0, /device:TPU:0, one launch (start us, length us, event | category | flops | bytes accessed | tf_op | source)
XLA Modules:
  0.0 140.0 jit_solution(4159584743243929971)
XLA Ops:
  6.5 0.8 broadcast_add_fusion.1
  7.3 0.8 copy.45
  8.1 0.8 slice_reduce_fusion.4
  8.9 0.8 slice_bitcast_fusion.14
  9.7 0.7 convert_divide_fusion
  10.4 0.2 multiply_convert_fusion.1
  10.6 0.3 fusion
  11.6 63.8 %all-reduce.2 = bf16[16,2048]{1,0:T(8,128)(2,1)S(1)} all-reduce(f32[16,2048]{1,0:T(8,128)S(1)} %bitcast.78), channel_id=3, replica_groups=mesh['pb'=2,'ka'=16] {'ka'}, use_global_device_ids=true, to_apply=%region_0.1.clone | all-reduce | flops 32768 | bytes 196608
  75.4 0.6 dynamic-slice.2
  76.0 0.7 fusion.28
  76.6 4.4 %all-gather.2 = bf16[2,1,2048]{2,1,0:T(2,128)(2,1)S(1)} all-gather(bf16[1,1,2048]{2,1,0:T(2,128)(2,1)S(1)} %fusion.28), channel_id=2, replica_groups=mesh['pb'=2,'ka'=16] {'pb'}, dimensions={0}, use_global_device_ids=true | all-gather | bytes 12288 | tf_op jit(solution)/shard_map/all_gather | solution.py:102
  81.8 17.5 %all-gather.1 = f32[16,1,2048]{2,1,0:T(1,128)S(1)} all-gather(f32[1,1,2048]{2,1,0:T(1,128)S(1)} %bitcast.80), channel_id=1, replica_groups=mesh['pb'=2,'ka'=16] {'ka'}, dimensions={0}, use_global_device_ids=true | all-gather | bytes 139264 | tf_op jit(solution)/shard_map/all_gather | solution.py:105
  99.3 0.3 fusion.15
  99.8 0.6 convolution_bitcast_fusion.1
  100.4 0.6 convolution_bitcast_fusion
  101.1 0.7 fusion.13
  101.8 0.7 fusion.9
  102.5 0.7 fusion.2
  103.2 19.1 %all-gather.3 = f32[16,1,32]{2,1,0:T(1,128)S(1)} all-gather(f32[1,1,32]{2,1,0:T(1,128)S(1)} %bitcast.83), channel_id=1, replica_groups=mesh['pb'=2,'ka'=16] {'ka'}, dimensions={0}, use_global_device_ids=true | all-gather | bytes 2176 | tf_op jit(solution)/shard_map/all_gather | solution.py:106
  122.2 0.2 add_divide_fusion
  122.9 1.0 fusion.6
  123.8 0.7 copy.55
  124.5 7.3 %reduce-scatter.4.cloned.1.call-done = f32[16,1]{1,0:T(8,128)} async-done(((f32[32,1]{1,0:T(8,128)}), f32[16,1]{1,0:T(8,128)}) %reduce-scatter.4.cloned.1.call-update) | async-done | bytes 80
  131.9 1.3 copy.56
  (35 shorter events, 2.0 us)
Async XLA Ops:
  6.5 4.1 %copy-start = (bf16[320,1,2048]{2,0,1:T(8,128)(2,1)S(1)}, bf16[320,1,2048]{2,0,1:T(8,128)(2,1)}, u32[]{:S(2)}) copy-start(bf16[320,1,2048]{2,0,1:T(8,128)(2,1)} %param.9) | copy-start | bytes 3932164
  6.5 125.3 %reduce-scatter.4.cloned.1.call-start = ((), (), s32[]{:S(2)}) async-start(), calls=%async_computation.1 | async-start | bytes 24576
  10.9 64.4 %copy-start.5 = (u32[32]{0:T(128)S(1)}, u32[32]{0:T(128)}, u32[]{:S(2)}) copy-start(u32[32]{0:T(128)} %constant.68) | copy-start | bytes 388
  10.9 70.2 %copy-start.1 = (f32[1,2048]{1,0:T(1,128)S(1)}, f32[1,2048]{1,0:T(1,128)}, u32[]{:S(2)}) copy-start(f32[1,2048]{1,0:T(1,128)} %param.10) | copy-start | bytes 24580
  11.0 88.3 %copy-start.4 = (s32[1,12]{1,0:T(1,128)S(1)}, s32[1,12]{1,0:T(1,128)}, u32[]{:S(2)}) copy-start(s32[1,12]{1,0:T(1,128)} %param.15) | copy-start | bytes 148
  11.2 88.6 %copy-start.2 = (f32[12,2,2]{0,2,1:T(2,128)S(1)}, f32[12,2,2]{0,2,1:T(2,128)}, u32[]{:S(2)}) copy-start(f32[12,2,2]{0,2,1:T(2,128)} %param.17) | copy-start | bytes 580
  101.8 1.4 copy-start.3
Sparse Core Ops, SparseCore 0:
  124.7 7.1 reduce-scatter.3
where the time goes:
time: 140 us
  blocking collectives  105 us (75%)
  between operations  13.6 us (10%)
  waiting for transfers between devices  7.35 us (5%)
  local copies, waits for them, and re-layouts  6.51 us (5%)
  matrix products  5.57 us (4%)
  other arithmetic  2.19 us (2%)
    unnamed x1, blocking collectives  63.8 us
    all_gather x1, blocking collectives, shards(): lax.all_gather(energies, 'ka', axis=0, tiled=True)  19.1 us
    all_gather x1, blocking collectives, shards(): lax.all_gather(eigvec, 'ka', axis=0, tiled=True)  17.5 us
    unnamed x2, waiting for transfers between devices  7.35 us
    all_gather x1, blocking collectives, shards(): wannier = lax.all_gather(own_wannier, 'pb', axis=1, tiled=True)  4.36 us
    unnamed x18, local copies, waits for them, and re-layouts  4.06 us
  transfers between devices with their start and end apart: 1, of which 1 were waited for; matrix products, arithmetic and copies ran while one was open for 0% of the time, Pallas kernels for 0%

commit v1 on v0

--- a/solution.py
+++ b/solution.py
@@ -8,6 +8,22 @@
 THERMAL = 0.1
 SMEARING = 0.05
 HIGHEST = lax.Precision.HIGHEST
+
+
+def collect(x, axis, dim):
+    ways, here, step = (lax.axis_size(axis), lax.axis_index(axis), x.shape[dim])
+    shape = [n * ways if d == dim else n for d, n in enumerate(x.shape)]
+    full = lax.dynamic_update_slice_in_dim(jnp.zeros(shape, x.dtype), x, here * step, axis=dim)
+    going_up = going_down = x
+    for far in range(1, ways // 2 + 1):
+        going_up = lax.ppermute(going_up, axis, [(d, (d + 1) % ways) for d in range(ways)])
+        full = lax.dynamic_update_slice_in_dim(full, going_up, (here - far) % ways * step, axis=dim)
+        if 2 * far < ways:
+            going_down = lax.ppermute(going_down, axis, [(d, (d - 1) % ways) for d in range(ways)])
+            full = lax.dynamic_update_slice_in_dim(
+                full, going_down, (here + far) % ways * step, axis=dim
+            )
+    return full
 
 
 def phases(k_coords, r_coords, degeneracy):
@@ -101,10 +117,7 @@
     own_wannier = partial_value.astype(jnp.bfloat16).reshape(points, local_modes, 2 * bands * bands)
     wannier = lax.all_gather(own_wannier, "pb", axis=1, tiled=True)
     pairs = kq_index.reshape(-1)
-    pieces = (
-        lax.all_gather(eigvec, "ka", axis=0, tiled=True),
-        lax.all_gather(energies, "ka", axis=0, tiled=True),
-    )
+    pieces = (lax.all_gather(eigvec, "ka", axis=0, tiled=True), collect(energies, "ka", 0))
     labels = jnp.arange(pieces[0].shape[0], dtype=jnp.int32)
     hits = (pairs[:, None] == labels[None, :]).astype(jnp.float32)
     vectors_sum = jnp.dot(hits, pieces[0], precision=HIGHEST, preferred_element_type=jnp.float32)

time: 140 us -> 163 us (1.16)
  starting transfers between devices: 0.01 us -> 32 us
  blocking collectives: 105 us -> 80.8 us
  waiting for transfers between devices: 7.35 us -> 20.4 us
    ppermute x0 -> x15, starting transfers between devices: none -> 32 us  [the longest x7 31.1 us: collect(): lax.ppermute(going_down, axis, [(d, (d - 1) % ways) for d in range(ways)])]
    all_gather x1 -> x0, blocking collectives: 19.1 us -> none  [shards(): lax.all_gather(energies, 'ka', axis=0, tiled=True)]
    ppermute x0 -> x15, waiting for transfers between devices: none -> 13 us  [the longest x8 12.8 us: collect(): lax.ppermute(going_up, axis, [(d, (d + 1) % ways) for d in range(ways)])]
    unnamed x1, blocking collectives: 63.8 us -> 59 us
  transfers between devices with their start and end apart: 1 -> 16, of which waited for: 1 -> 8; matrix products, arithmetic and copies ran while one was open for 0% -> 7% of each run, Pallas kernels for 0% -> 0%
where the time goes in v1:
time: 163 us; the launch traced here: 162 us
  blocking collectives  80.8 us (50%)
  starting transfers between devices  32 us (20%)
  waiting for transfers between devices  20.4 us (13%)
  between operations  13.7 us (8%)
  local copies, waits for them, and re-layouts  7.64 us (5%)
  matrix products  5.56 us (3%)
  other arithmetic  2.09 us (1%)
    unnamed x1, blocking collectives  59 us
    ppermute x7, starting transfers between devices, collect(): lax.ppermute(going_down, axis, [(d, (d - 1) % ways) for d in range(ways)])  31.1 us
    all_gather x1, blocking collectives, shards(): lax.all_gather(eigvec, 'ka', axis=0, tiled=True)  17.5 us
    ppermute x8, waiting for transfers between devices, collect(): lax.ppermute(going_up, axis, [(d, (d + 1) % ways) for d in range(ways)])  12.8 us
    unnamed x2, waiting for transfers between devices  7.37 us
    all_gather x1, blocking collectives, shards(): wannier = lax.all_gather(own_wannier, 'pb', axis=1, tiled=True)  4.36 us
    unnamed x18, local copies, waits for them, and re-layouts  4.07 us
  transfers between devices with their start and end apart: 16, of which 8 were waited for; matrix products, arithmetic and copies ran while one was open for 7% of the time, Pallas kernels for 0%

profile of v1, /device:TPU:0, one launch (start us, length us, event | category | flops | bytes accessed | tf_op | source)
XLA Modules:
  0.0 162.2 jit_solution(8904176005077034815)
XLA Ops:
  7.0 5.0 %collective-permute-start.1 = (f32[1,32]{1,0:T(1,128)}, f32[1,32]{1,0:T(1,128)S(1)}, u32[]{:S(2)}, u32[]{:S(2)}) collective-permute-start(f32[1,32]{1,0:T(1,128)} %param.11), channel_id=1, source_target_pairs={{0,15},{1,0},{2,1},{3,2},{4,3},{5,4},{6,5},{7,6},{8,7},{9,8},{10,9... | collective-permute-start | bytes 392 | tf_op jit(solution)/shard_map/ppermute | solution.py:22
  12.7 0.8 copy.45
  13.5 0.7 slice_reduce_fusion.1
  15.0 0.8 slice_reduce_fusion.4
  15.8 0.8 slice_bitcast_fusion.14
  17.7 59.0 %all-reduce.2 = bf16[16,2048]{1,0:T(8,128)(2,1)S(1)} all-reduce(f32[16,2048]{1,0:T(8,128)S(1)} %bitcast.76), channel_id=3, replica_groups=mesh['pb'=2,'ka'=16] {'ka'}, use_global_device_ids=true, to_apply=%region_0.1.clone | all-reduce | flops 32768 | bytes 196608
  78.0 4.4 %all-gather.2 = bf16[2,1,2048]{2,1,0:T(2,128)(2,1)S(1)} all-gather(bf16[1,1,2048]{2,1,0:T(2,128)(2,1)S(1)} %fusion.28), channel_id=2, replica_groups=mesh['pb'=2,'ka'=16] {'pb'}, dimensions={0}, use_global_device_ids=true | all-gather | bytes 12288 | tf_op jit(solution)/shard_map/all_gather | solution.py:118
  83.0 17.5 %all-gather.1 = f32[16,1,2048]{2,1,0:T(1,128)S(1)} all-gather(f32[1,1,2048]{2,1,0:T(1,128)S(1)} %bitcast.78), channel_id=1, replica_groups=mesh['pb'=2,'ka'=16] {'ka'}, dimensions={0}, use_global_device_ids=true | all-gather | bytes 139264 | tf_op jit(solution)/shard_map/all_gather | solution.py:120
  105.1 4.1 %collective-permute-start.3 = (f32[1,32]{1,0:T(1,128)S(1)}, f32[1,32]{1,0:T(1,128)S(1)}, u32[]{:S(2)}, u32[]{:S(2)}) collective-permute-start(f32[1,32]{1,0:T(1,128)S(1)} %collective-permute-done.1), channel_id=1, source_target_pairs={{0,15},{1,0},{2,1},{3,2},{4,3},{5,4},{6,5},{7,6},{8,7},{9,8},{10,9... | collective-permute-start | bytes 392 | tf_op jit(solution)/shard_map/ppermute | solution.py:22
  109.3 1.2 collective-permute-done.2
  110.5 4.4 %collective-permute-start.5 = (f32[1,32]{1,0:T(1,128)S(1)}, f32[1,32]{1,0:T(1,128)S(1)}, u32[]{:S(2)}, u32[]{:S(2)}) collective-permute-start(f32[1,32]{1,0:T(1,128)S(1)} %collective-permute-done.3), channel_id=1, source_target_pairs={{0,15},{1,0},{2,1},{3,2},{4,3},{5,4},{6,5},{7,6},{8,7},{9,8},{10,9... | collective-permute-start | bytes 392 | tf_op jit(solution)/shard_map/ppermute | solution.py:22
  115.0 1.2 collective-permute-done.4
  116.2 4.4 %collective-permute-start.7 = (f32[1,32]{1,0:T(1,128)S(1)}, f32[1,32]{1,0:T(1,128)S(1)}, u32[]{:S(2)}, u32[]{:S(2)}) collective-permute-start(f32[1,32]{1,0:T(1,128)S(1)} %collective-permute-done.5), channel_id=1, source_target_pairs={{0,15},{1,0},{2,1},{3,2},{4,3},{5,4},{6,5},{7,6},{8,7},{9,8},{10,9... | collective-permute-start | bytes 392 | tf_op jit(solution)/shard_map/ppermute | solution.py:22
  120.7 1.2 collective-permute-done.6
  121.9 4.4 %collective-permute-start.9 = (f32[1,32]{1,0:T(1,128)S(1)}, f32[1,32]{1,0:T(1,128)S(1)}, u32[]{:S(2)}, u32[]{:S(2)}) collective-permute-start(f32[1,32]{1,0:T(1,128)S(1)} %collective-permute-done.7), channel_id=1, source_target_pairs={{0,15},{1,0},{2,1},{3,2},{4,3},{5,4},{6,5},{7,6},{8,7},{9,8},{10,9... | collective-permute-start | bytes 392 | tf_op jit(solution)/shard_map/ppermute | solution.py:22
  126.4 1.2 collective-permute-done.8
  127.6 4.4 %collective-permute-start.11 = (f32[1,32]{1,0:T(1,128)S(1)}, f32[1,32]{1,0:T(1,128)S(1)}, u32[]{:S(2)}, u32[]{:S(2)}) collective-permute-start(f32[1,32]{1,0:T(1,128)S(1)} %collective-permute-done.9), channel_id=1, source_target_pairs={{0,15},{1,0},{2,1},{3,2},{4,3},{5,4},{6,5},{7,6},{8,7},{9,8},{10,9... | collective-permute-start | bytes 392 | tf_op jit(solution)/shard_map/ppermute | solution.py:22
  132.1 1.2 collective-permute-done.10
  133.3 4.4 %collective-permute-start.13 = (f32[1,32]{1,0:T(1,128)S(1)}, f32[1,32]{1,0:T(1,128)S(1)}, u32[]{:S(2)}, u32[]{:S(2)}) collective-permute-start(f32[1,32]{1,0:T(1,128)S(1)} %collective-permute-done.11), channel_id=1, source_target_pairs={{0,15},{1,0},{2,1},{3,2},{4,3},{5,4},{6,5},{7,6},{8,7},{9,8},{10,9... | collective-permute-start | bytes 392 | tf_op jit(solution)/shard_map/ppermute | solution.py:22
  137.7 1.2 collective-permute-done.12
  139.0 5.6 %collective-permute-done.14 = f32[1,32]{1,0:T(1,128)S(1)} collective-permute-done((f32[1,32]{1,0:T(1,128)S(1)}, f32[1,32]{1,0:T(1,128)S(1)}, u32[]{:S(2)}, u32[]{:S(2)}) %collective-permute-start.14) | collective-permute-done | bytes 160 | tf_op jit(solution)/shard_map/ppermute | solution.py:19
  145.1 0.9 fusion.6
  146.8 7.4 %reduce-scatter.4.cloned.1.call-done = f32[16,1]{1,0:T(8,128)} async-done(((f32[32,1]{1,0:T(8,128)}), f32[16,1]{1,0:T(8,128)}) %reduce-scatter.4.cloned.1.call-update) | async-done | bytes 80
  154.1 1.3 copy.56
  (81 shorter events, 11.1 us)
Async XLA Ops:
  6.5 10.3 %copy-start = (bf16[320,1,2048]{2,0,1:T(8,128)(2,1)S(1)}, bf16[320,1,2048]{2,0,1:T(8,128)(2,1)}, u32[]{:S(2)}) copy-start(bf16[320,1,2048]{2,0,1:T(8,128)(2,1)} %param.9) | copy-start | bytes 3932164
  6.5 147.6 %reduce-scatter.4.cloned.1.call-start = ((), (), s32[]{:S(2)}) async-start(), calls=%async_computation.1 | async-start | bytes 24576
  6.5 98.2 %collective-permute-start = (f32[1,32]{1,0:T(1,128)}, f32[1,32]{1,0:T(1,128)S(1)}, u32[]{:S(2)}, u32[]{:S(2)}) collective-permute-start(f32[1,32]{1,0:T(1,128)} %param.11), channel_id=1, source_target_pairs={{0,1},{1,2},{2,3},{3,4},{4,5},{5,6},{6,7},{7,8},{8,9},{9,10},{10,1... | collective-permute-start | bytes 392 | tf_op jit(solution)/shard_map/ppermute | solution.py:19
  7.0 98.1 %collective-permute-start.1 = (f32[1,32]{1,0:T(1,128)}, f32[1,32]{1,0:T(1,128)S(1)}, u32[]{:S(2)}, u32[]{:S(2)}) collective-permute-start(f32[1,32]{1,0:T(1,128)} %param.11), channel_id=1, source_target_pairs={{0,15},{1,0},{2,1},{3,2},{4,3},{5,4},{6,5},{7,6},{8,7},{9,8},{10,9... | collective-permute-start | bytes 392 | tf_op jit(solution)/shard_map/ppermute | solution.py:22
  17.1 59.6 %copy-start.5 = (u32[32]{0:T(128)S(1)}, u32[32]{0:T(128)}, u32[]{:S(2)}) copy-start(u32[32]{0:T(128)} %constant.172) | copy-start | bytes 388
  17.1 65.9 %copy-start.1 = (f32[1,2048]{1,0:T(1,128)S(1)}, f32[1,2048]{1,0:T(1,128)}, u32[]{:S(2)}) copy-start(f32[1,2048]{1,0:T(1,128)} %param.10) | copy-start | bytes 24580
  17.1 83.4 %copy-start.4 = (s32[1,12]{1,0:T(1,128)S(1)}, s32[1,12]{1,0:T(1,128)}, u32[]{:S(2)}) copy-start(s32[1,12]{1,0:T(1,128)} %param.15) | copy-start | bytes 148
  17.4 83.7 %copy-start.2 = (f32[12,2,2]{0,2,1:T(2,128)S(1)}, f32[12,2,2]{0,2,1:T(2,128)}, u32[]{:S(2)}) copy-start(f32[12,2,2]{0,2,1:T(2,128)} %param.17) | copy-start | bytes 580
  103.0 1.6 copy-start.3
  104.7 5.7 %collective-permute-start.2 = (f32[1,32]{1,0:T(1,128)S(1)}, f32[1,32]{1,0:T(1,128)S(1)}, u32[]{:S(2)}, u32[]{:S(2)}) collective-permute-start(f32[1,32]{1,0:T(1,128)S(1)} %collective-permute-done), channel_id=1, source_target_pairs={{0,1},{1,2},{2,3},{3,4},{4,5},{5,6},{6,7},{7,8},{8,9},{9,10},{10,1... | collective-permute-start | bytes 392 | tf_op jit(solution)/shard_map/ppermute | solution.py:19
  105.1 5.4 %collective-permute-start.3 = (f32[1,32]{1,0:T(1,128)S(1)}, f32[1,32]{1,0:T(1,128)S(1)}, u32[]{:S(2)}, u32[]{:S(2)}) collective-permute-start(f32[1,32]{1,0:T(1,128)S(1)} %collective-permute-done.1), channel_id=1, source_target_pairs={{0,15},{1,0},{2,1},{3,2},{4,3},{5,4},{6,5},{7,6},{8,7},{9,8},{10,9... | collective-permute-start | bytes 392 | tf_op jit(solution)/shard_map/ppermute | solution.py:22
  110.5 5.7 %collective-permute-start.4 = (f32[1,32]{1,0:T(1,128)S(1)}, f32[1,32]{1,0:T(1,128)S(1)}, u32[]{:S(2)}, u32[]{:S(2)}) collective-permute-start(f32[1,32]{1,0:T(1,128)S(1)} %collective-permute-done.2), channel_id=1, source_target_pairs={{0,1},{1,2},{2,3},{3,4},{4,5},{5,6},{6,7},{7,8},{8,9},{9,10},{10,1... | collective-permute-start | bytes 392 | tf_op jit(solution)/shard_map/ppermute | solution.py:19
  110.5 5.7 %collective-permute-start.5 = (f32[1,32]{1,0:T(1,128)S(1)}, f32[1,32]{1,0:T(1,128)S(1)}, u32[]{:S(2)}, u32[]{:S(2)}) collective-permute-start(f32[1,32]{1,0:T(1,128)S(1)} %collective-permute-done.3), channel_id=1, source_target_pairs={{0,15},{1,0},{2,1},{3,2},{4,3},{5,4},{6,5},{7,6},{8,7},{9,8},{10,9... | collective-permute-start | bytes 392 | tf_op jit(solution)/shard_map/ppermute | solution.py:22
  116.2 5.7 %collective-permute-start.6 = (f32[1,32]{1,0:T(1,128)S(1)}, f32[1,32]{1,0:T(1,128)S(1)}, u32[]{:S(2)}, u32[]{:S(2)}) collective-permute-start(f32[1,32]{1,0:T(1,128)S(1)} %collective-permute-done.4), channel_id=1, source_target_pairs={{0,1},{1,2},{2,3},{3,4},{4,5},{5,6},{6,7},{7,8},{8,9},{9,10},{10,1... | collective-permute-start | bytes 392 | tf_op jit(solution)/shard_map/ppermute | solution.py:19
  116.2 5.7 %collective-permute-start.7 = (f32[1,32]{1,0:T(1,128)S(1)}, f32[1,32]{1,0:T(1,128)S(1)}, u32[]{:S(2)}, u32[]{:S(2)}) collective-permute-start(f32[1,32]{1,0:T(1,128)S(1)} %collective-permute-done.5), channel_id=1, source_target_pairs={{0,15},{1,0},{2,1},{3,2},{4,3},{5,4},{6,5},{7,6},{8,7},{9,8},{10,9... | collective-permute-start | bytes 392 | tf_op jit(solution)/shard_map/ppermute | solution.py:22
  121.9 5.7 %collective-permute-start.8 = (f32[1,32]{1,0:T(1,128)S(1)}, f32[1,32]{1,0:T(1,128)S(1)}, u32[]{:S(2)}, u32[]{:S(2)}) collective-permute-start(f32[1,32]{1,0:T(1,128)S(1)} %collective-permute-done.6), channel_id=1, source_target_pairs={{0,1},{1,2},{2,3},{3,4},{4,5},{5,6},{6,7},{7,8},{8,9},{9,10},{10,1... | collective-permute-start | bytes 392 | tf_op jit(solution)/shard_map/ppermute | solution.py:19
  121.9 5.7 %collective-permute-start.9 = (f32[1,32]{1,0:T(1,128)S(1)}, f32[1,32]{1,0:T(1,128)S(1)}, u32[]{:S(2)}, u32[]{:S(2)}) collective-permute-start(f32[1,32]{1,0:T(1,128)S(1)} %collective-permute-done.7), channel_id=1, source_target_pairs={{0,15},{1,0},{2,1},{3,2},{4,3},{5,4},{6,5},{7,6},{8,7},{9,8},{10,9... | collective-permute-start | bytes 392 | tf_op jit(solution)/shard_map/ppermute | solution.py:22
  127.6 5.7 %collective-permute-start.10 = (f32[1,32]{1,0:T(1,128)S(1)}, f32[1,32]{1,0:T(1,128)S(1)}, u32[]{:S(2)}, u32[]{:S(2)}) collective-permute-start(f32[1,32]{1,0:T(1,128)S(1)} %collective-permute-done.8), channel_id=1, source_target_pairs={{0,1},{1,2},{2,3},{3,4},{4,5},{5,6},{6,7},{7,8},{8,9},{9,10},{10,1... | collective-permute-start | bytes 392 | tf_op jit(solution)/shard_map/ppermute | solution.py:19
  127.6 5.7 %collective-permute-start.11 = (f32[1,32]{1,0:T(1,128)S(1)}, f32[1,32]{1,0:T(1,128)S(1)}, u32[]{:S(2)}, u32[]{:S(2)}) collective-permute-start(f32[1,32]{1,0:T(1,128)S(1)} %collective-permute-done.9), channel_id=1, source_target_pairs={{0,15},{1,0},{2,1},{3,2},{4,3},{5,4},{6,5},{7,6},{8,7},{9,8},{10,9... | collective-permute-start | bytes 392 | tf_op jit(solution)/shard_map/ppermute | solution.py:22
  133.2 5.7 %collective-permute-start.12 = (f32[1,32]{1,0:T(1,128)S(1)}, f32[1,32]{1,0:T(1,128)S(1)}, u32[]{:S(2)}, u32[]{:S(2)}) collective-permute-start(f32[1,32]{1,0:T(1,128)S(1)} %collective-permute-done.10), channel_id=1, source_target_pairs={{0,1},{1,2},{2,3},{3,4},{4,5},{5,6},{6,7},{7,8},{8,9},{9,10},{10,1... | collective-permute-start | bytes 392 | tf_op jit(solution)/shard_map/ppermute | solution.py:19
  133.3 5.7 %collective-permute-start.13 = (f32[1,32]{1,0:T(1,128)S(1)}, f32[1,32]{1,0:T(1,128)S(1)}, u32[]{:S(2)}, u32[]{:S(2)}) collective-permute-start(f32[1,32]{1,0:T(1,128)S(1)} %collective-permute-done.11), channel_id=1, source_target_pairs={{0,15},{1,0},{2,1},{3,2},{4,3},{5,4},{6,5},{7,6},{8,7},{9,8},{10,9... | collective-permute-start | bytes 392 | tf_op jit(solution)/shard_map/ppermute | solution.py:22
  138.9 5.7 %collective-permute-start.14 = (f32[1,32]{1,0:T(1,128)S(1)}, f32[1,32]{1,0:T(1,128)S(1)}, u32[]{:S(2)}, u32[]{:S(2)}) collective-permute-start(f32[1,32]{1,0:T(1,128)S(1)} %collective-permute-done.12), channel_id=1, source_target_pairs={{0,1},{1,2},{2,3},{3,4},{4,5},{5,6},{6,7},{7,8},{8,9},{9,10},{10,1... | collective-permute-start | bytes 392 | tf_op jit(solution)/shard_map/ppermute | solution.py:19
Sparse Core Ops, SparseCore 0:
  146.9 7.1 reduce-scatter.3
